TPU v7x, 256 devices: a whole 4x4x8 slice. The times are simulated.
256 devices in a mesh: dp: 32 (over z, y_hi, core), fsdp: 8 (over y_lo, x).
Axes of the slice: x: 4, y: 4 (y_hi: 2, y_lo: 2; y = y_hi * 2 + y_lo), z: 8, core: 2. Of those that a mesh axis runs over, the one named last changes fastest.
Arguments:
- hidden: bfloat16 [131072, 1152], P(('dp', 'fsdp')), may hold values from -6 to 6
- text_ids: int32 [8192, 16], P(('dp', 'fsdp')), may hold values from 0 to 31999, as said below
- ln_gain: float32 [1152], replicated, may hold values from 0.5 to 1.5
- ln_bias: float32 [1152], replicated, may hold values from -2 to 2
- fc1_weight: bfloat16 [1152, 4304], P(None, 'fsdp'), may hold values from -0.1875 to 0.1875
- fc1_bias: float32 [4304], replicated, may hold values from -3 to 3
- fc2_weight: bfloat16 [4304, 1152], P('fsdp'), may hold values from -0.09375 to 0.09375
- fc2_bias: float32 [1152], replicated, may hold values from -3 to 3
- final_gain: float32 [1152], replicated, may hold values from 0.5 to 1.5
- final_bias: float32 [1152], replicated, may hold values from -0.2 to 0.2
- head_weight: bfloat16 [1152, 1152], replicated, may hold values from -0.1875 to 0.1875
- head_bias: float32 [1152], replicated, may hold values from -0.3 to 0.3
- image_emb: bfloat16 [8192, 1152], P(('dp', 'fsdp')), may hold values from -6 to 6
- teacher_logits: bfloat16 [8192, 12, 256], P('dp', None, 'fsdp'), may hold values from -12 to 12
- logit_scale: float32 [1], replicated, may hold values from 4 to 16
- logit_bias: float32 [1], replicated, may hold values from -3 to 0
Outputs:
- image_grad: float32 [8192, 1152], P(('dp', 'fsdp'))
Inputs may be any that keep to these rules, and one draw needn't show every extreme that they name: `text_ids`: 0 marks padding after a text's end; every text has at least one token and the tokens of a text come first.
All inputs are finite; a program needn't handle non-finite values.
Results may differ from a plain program's by a relative error of at most 0.0018.
Values may be sent and summed in bfloat16 or wider, within the bound.
No kernel may reach another device: no remote copies, remote signals or barrier semaphores. Data moves between devices by JAX's collectives and lax.ppermute only.
A program may use at most 128 MiB of HBM per device.

v0:
```python
import jax
import jax.numpy as jnp
from jax import lax
from jax.sharding import PartitionSpec as P


def from_everyone(array, axis):
    copies = jnp.broadcast_to(array, (lax.axis_size(axis), *array.shape))
    return lax.all_to_all(copies, axis, split_axis=0, concat_axis=0, tiled=True)


def joined_along(parts, dim):
    parts = jnp.moveaxis(parts, 0, dim)
    dims = parts.shape
    return parts.reshape(*dims[:dim], dims[dim] * dims[dim + 1], *dims[dim + 2 :])


def gather_directly(array, axis, dim):
    parts = from_everyone(array, axis)
    return joined_along(parts, dim)


def from_behind(array, axis, by):
    count = lax.axis_size(axis)
    return lax.ppermute(array, axis, [(i, (i + by) % count) for i in range(count)])


def layer_norm(values, gain, shift):
    centre = jnp.mean(values, axis=-1, keepdims=True)
    spread = jnp.mean((values - centre) ** 2, axis=-1, keepdims=True)
    return (values - centre) * lax.rsqrt(spread + 1e-06) * gain + shift


def on_device(
    hidden,
    text_ids,
    ln_gain,
    ln_bias,
    fc1_weight,
    fc1_bias,
    fc2_weight,
    fc2_bias,
    final_gain,
    final_bias,
    head_weight,
    head_bias,
    image_emb,
    teacher_logits,
    logit_scale,
    logit_bias,
):
    width = hidden.shape[1]
    texts_here, seq_len = text_ids.shape
    window = teacher_logits.shape[1]
    flat = hidden.astype(jnp.float32)
    normed = layer_norm(flat, ln_gain, ln_bias).astype(jnp.bfloat16)
    pre = (
        jnp.dot(
            normed,
            lax.all_gather(fc1_weight, "fsdp", axis=1, tiled=True),
            preferred_element_type=jnp.float32,
        )
        + fc1_bias
    )
    act = jax.nn.gelu(pre, approximate=True).astype(jnp.bfloat16)
    mixed = jnp.dot(
        act,
        lax.all_gather(fc2_weight, "fsdp", axis=0, tiled=True),
        preferred_element_type=jnp.float32,
    )
    out = flat + mixed + fc2_bias
    final = layer_norm(out, final_gain, final_bias).reshape(texts_here, seq_len, width)
    keep = (text_ids != 0).astype(jnp.float32)
    pooled = jnp.sum(final * keep[:, :, None], axis=1) / jnp.sum(keep, axis=1)[:, None]
    emb = (
        jnp.dot(pooled.astype(jnp.bfloat16), head_weight, preferred_element_type=jnp.float32)
        + head_bias
    )
    text_unit = (emb * lax.rsqrt(jnp.sum(emb * emb, axis=-1, keepdims=True) + 1e-06)).astype(
        jnp.bfloat16
    )
    group_units = gather_directly(text_unit, "fsdp", 0)
    images = image_emb.astype(jnp.float32)
    image_unit = (
        images * lax.rsqrt(jnp.sum(images * images, axis=-1, keepdims=True) + 1e-06)
    ).astype(jnp.bfloat16)
    scale = logit_scale[0]
    offset = logit_bias[0]

    def pair_term(units, pictures, tile):
        score = (
            scale
            * lax.dot_general(
                units, pictures, (((1,), (1,)), ((), ())), preferred_element_type=jnp.float32
            )
            + offset
        )
        weight = (jax.nn.sigmoid(score) - jax.nn.sigmoid(tile.astype(jnp.float32))).astype(
            jnp.bfloat16
        )
        return lax.dot_general(
            weight, units, (((0,), (0,)), ((), ())), preferred_element_type=jnp.float32
        )

    start_grad = jnp.zeros(image_unit.shape, jnp.float32)

    def turn_images(step, carry):
        pictures, total = carry
        tile = lax.dynamic_index_in_dim(teacher_logits, step, 1, keepdims=False)
        total = total + pair_term(group_units, pictures, tile)
        pictures, total = (
            from_behind(pictures.astype(jnp.float32), "dp", -1).astype(pictures.dtype),
            from_behind(total, "dp", -1),
        )
        return (pictures, total)

    pictures, total = lax.fori_loop(0, window - 1, turn_images, (image_unit, start_grad))
    total = total + pair_term(group_units, pictures, teacher_logits[:, window - 1, :])
    total = from_behind(total, "dp", window - 1)
    return scale * total


def solution(mesh):
    placed = (
        P(("dp", "fsdp"), None),
        P(("dp", "fsdp"), None),
        P(),
        P(),
        P(None, "fsdp"),
        P(),
        P("fsdp", None),
        P(),
        P(),
        P(),
        P(),
        P(),
        P(("dp", "fsdp"), None),
        P("dp", None, "fsdp"),
        P(),
        P(),
    )
    return jax.shard_map(
        on_device, mesh=mesh, in_specs=placed, out_specs=P(("dp", "fsdp"), None), check_vma=False
    )
```

profile of v0, /device:TPU:1, one launch (start us, length us, event | category | flops | bytes accessed | tf_op | source)
XLA Modules:
  0.0 442.1 jit_solution(9942454543745646307)
XLA Ops:
  11.5 111.0 %all-gather.5.cloned.1.call-done = bf16[8,538,1152]{2,1,0:T(8,128)(2,1)} async-done(((bf16[1,538,1152]{2,1,0:T(8,128)(2,1)}), bf16[8,538,1152]{2,1,0:T(8,128)(2,1)}) %all-gather.5.cloned.1.call-update) | async-done | bytes 9916432 | tf_op jit(solution)/shard_map/all_gather | solution.py:60
  122.5 11.8 %reshape.68 = bf16[4304,1152]{1,0:T(8,128)(2,1)} reshape(bf16[8,538,1152]{2,1,0:T(8,128)(2,1)} %all-gather.5.cloned.1.call-done) | data formatting | bytes 19832832
  134.4 98.5 %all-gather.7.cloned.1.call-done = bf16[8,538,1152]{2,1,0:T(8,128)(2,1)} async-done(((bf16[1,538,1152]{2,1,0:T(8,128)(2,1)}), bf16[8,538,1152]{2,1,0:T(8,128)(2,1)}) %all-gather.7.cloned.1.call-update) | async-done | bytes 9916432 | tf_op jit(solution)/shard_map/all_gather | solution.py:68
  232.9 11.9 %reshape.70 = bf16[4304,1152]{1,0:T(8,128)(2,1)} reshape(bf16[8,538,1152]{2,1,0:T(8,128)(2,1)} %all-gather.7.cloned.1.call-done) | data formatting | bytes 19832832
  244.8 23.1 %fusion.72 = (f32[512]{0:T(512)S(1)}, f32[512,1152]{1,0:T(8,128)}) fusion(f32[1152]{0:T(1024)S(1)} %copy-done.8, bf16[4304,1152]{1,0:T(8,128)(2,1)} %reshape.70, bf16[4304,1152]{1,0:T(8,128)(2,1)} %reshape.68, f32[4304]{0:T(1024)S(1)} %copy-done.7, bf16[512,1152]{1,0:T(8,128)(2,1)} %param.18, f32[1152]{0:T(1024)S(1)} %copy-done.9, f32[1152]{0:T(1024)S(1)} %copy-done.10, ...), kind=kOutput, calls=%fused_computation.91 | convolution fusion | flops 10182344704 | bytes 23408960 | tf_op jit(solution)/shard_map/dot_general | solution.py:66
  272.9 3.5 all-to-all-start
  277.8 9.5 %all-to-all-done = bf16[8,32,1152]{2,1,0:T(8,128)(2,1)S(1)} async-done(((bf16[8,32,1152]{2,1,0:T(8,128)(2,1)}), bf16[8,32,1152]{2,1,0:T(8,128)(2,1)S(1)}, u32[]{:S(2)}, u32[]{:S(2)}) %all-to-all-start) | async-done | bytes 589856 | tf_op jit(solution)/shard_map/all_to_all | solution.py:9
  287.3 134.7 %while.15 = (s32[]{:T(128)}, bf16[32,1152]{1,0:T(8,128)(2,1)S(1)}, f32[32,1152]{1,0:T(8,128)S(1)}, f32[]{:T(128)}, bf16[256,1152]{1,0:T(8,128)(2,1)S(1)}, /*inde...) while((s32[]{:T(128)}, bf16[32,1152]{1,0:T(8,128)(2,1)S(1)}, f32[32,1152]{1,0:T(8,128)S(1)}, f32[]{:T(128)}, ...), condition=%wide.region_9.10_spmd, body=%wide.region_8.9_spmd.sunk | while | flops 37875712 | bytes 2598565 | solution.py:117
  287.4 3.3 convolution_add_fusion.4
  291.4 4.8 %collective-permute-start = (bf16[32,1152]{1,0:T(8,128)(2,1)S(1)}, bf16[32,1152]{1,0:T(8,128)(2,1)S(1)}, u32[]{:S(2)}, u32[]{:S(2)}) collective-permute-start(bf16[32,1152]{1,0:T(8,128)(2,1)S(1)} %copy.24), channel_id=1, source_target_pairs={{0,248},{8,0},{16,8},{24,16},{32,24},{40,32},{48,40},{56,48},{64,5... | collective-permute-start | bytes 221192 | tf_op jit(solution)/shard_map/while/body/eval_jaxpr/ppermute | solution.py:25
  297.7 3.3 convolution_add_fusion.4
  303.2 5.5 %collective-permute-start = (bf16[32,1152]{1,0:T(8,128)(2,1)S(1)}, bf16[32,1152]{1,0:T(8,128)(2,1)S(1)}, u32[]{:S(2)}, u32[]{:S(2)}) collective-permute-start(bf16[32,1152]{1,0:T(8,128)(2,1)S(1)} %copy.24), channel_id=1, source_target_pairs={{0,248},{8,0},{16,8},{24,16},{32,24},{40,32},{48,40},{56,48},{64,5... | collective-permute-start | bytes 221192 | tf_op jit(solution)/shard_map/while/body/eval_jaxpr/ppermute | solution.py:25
  309.7 3.3 convolution_add_fusion.4
  312.9 2.7 collective-permute-start.1
  315.7 5.5 %collective-permute-start = (bf16[32,1152]{1,0:T(8,128)(2,1)S(1)}, bf16[32,1152]{1,0:T(8,128)(2,1)S(1)}, u32[]{:S(2)}, u32[]{:S(2)}) collective-permute-start(bf16[32,1152]{1,0:T(8,128)(2,1)S(1)} %copy.24), channel_id=1, source_target_pairs={{0,248},{8,0},{16,8},{24,16},{32,24},{40,32},{48,40},{56,48},{64,5... | collective-permute-start | bytes 221192 | tf_op jit(solution)/shard_map/while/body/eval_jaxpr/ppermute | solution.py:25
  322.1 3.3 convolution_add_fusion.4
  328.2 5.5 %collective-permute-start = (bf16[32,1152]{1,0:T(8,128)(2,1)S(1)}, bf16[32,1152]{1,0:T(8,128)(2,1)S(1)}, u32[]{:S(2)}, u32[]{:S(2)}) collective-permute-start(bf16[32,1152]{1,0:T(8,128)(2,1)S(1)} %copy.24), channel_id=1, source_target_pairs={{0,248},{8,0},{16,8},{24,16},{32,24},{40,32},{48,40},{56,48},{64,5... | collective-permute-start | bytes 221192 | tf_op jit(solution)/shard_map/while/body/eval_jaxpr/ppermute | solution.py:25
  334.6 3.3 convolution_add_fusion.4
  340.7 5.5 %collective-permute-start = (bf16[32,1152]{1,0:T(8,128)(2,1)S(1)}, bf16[32,1152]{1,0:T(8,128)(2,1)S(1)}, u32[]{:S(2)}, u32[]{:S(2)}) collective-permute-start(bf16[32,1152]{1,0:T(8,128)(2,1)S(1)} %copy.24), channel_id=1, source_target_pairs={{0,248},{8,0},{16,8},{24,16},{32,24},{40,32},{48,40},{56,48},{64,5... | collective-permute-start | bytes 221192 | tf_op jit(solution)/shard_map/while/body/eval_jaxpr/ppermute | solution.py:25
  347.1 3.3 convolution_add_fusion.4
  353.1 5.5 %collective-permute-start = (bf16[32,1152]{1,0:T(8,128)(2,1)S(1)}, bf16[32,1152]{1,0:T(8,128)(2,1)S(1)}, u32[]{:S(2)}, u32[]{:S(2)}) collective-permute-start(bf16[32,1152]{1,0:T(8,128)(2,1)S(1)} %copy.24), channel_id=1, source_target_pairs={{0,248},{8,0},{16,8},{24,16},{32,24},{40,32},{48,40},{56,48},{64,5... | collective-permute-start | bytes 221192 | tf_op jit(solution)/shard_map/while/body/eval_jaxpr/ppermute | solution.py:25
  359.6 3.3 convolution_add_fusion.4
  365.6 5.5 %collective-permute-start = (bf16[32,1152]{1,0:T(8,128)(2,1)S(1)}, bf16[32,1152]{1,0:T(8,128)(2,1)S(1)}, u32[]{:S(2)}, u32[]{:S(2)}) collective-permute-start(bf16[32,1152]{1,0:T(8,128)(2,1)S(1)} %copy.24), channel_id=1, source_target_pairs={{0,248},{8,0},{16,8},{24,16},{32,24},{40,32},{48,40},{56,48},{64,5... | collective-permute-start | bytes 221192 | tf_op jit(solution)/shard_map/while/body/eval_jaxpr/ppermute | solution.py:25
  372.1 3.3 convolution_add_fusion.4
  378.1 5.5 %collective-permute-start = (bf16[32,1152]{1,0:T(8,128)(2,1)S(1)}, bf16[32,1152]{1,0:T(8,128)(2,1)S(1)}, u32[]{:S(2)}, u32[]{:S(2)}) collective-permute-start(bf16[32,1152]{1,0:T(8,128)(2,1)S(1)} %copy.24), channel_id=1, source_target_pairs={{0,248},{8,0},{16,8},{24,16},{32,24},{40,32},{48,40},{56,48},{64,5... | collective-permute-start | bytes 221192 | tf_op jit(solution)/shard_map/while/body/eval_jaxpr/ppermute | solution.py:25
  384.6 3.3 convolution_add_fusion.4
  390.6 5.5 %collective-permute-start = (bf16[32,1152]{1,0:T(8,128)(2,1)S(1)}, bf16[32,1152]{1,0:T(8,128)(2,1)S(1)}, u32[]{:S(2)}, u32[]{:S(2)}) collective-permute-start(bf16[32,1152]{1,0:T(8,128)(2,1)S(1)} %copy.24), channel_id=1, source_target_pairs={{0,248},{8,0},{16,8},{24,16},{32,24},{40,32},{48,40},{56,48},{64,5... | collective-permute-start | bytes 221192 | tf_op jit(solution)/shard_map/while/body/eval_jaxpr/ppermute | solution.py:25
  397.1 3.3 convolution_add_fusion.4
  403.1 5.5 %collective-permute-start = (bf16[32,1152]{1,0:T(8,128)(2,1)S(1)}, bf16[32,1152]{1,0:T(8,128)(2,1)S(1)}, u32[]{:S(2)}, u32[]{:S(2)}) collective-permute-start(bf16[32,1152]{1,0:T(8,128)(2,1)S(1)} %copy.24), channel_id=1, source_target_pairs={{0,248},{8,0},{16,8},{24,16},{32,24},{40,32},{48,40},{56,48},{64,5... | collective-permute-start | bytes 221192 | tf_op jit(solution)/shard_map/while/body/eval_jaxpr/ppermute | solution.py:25
  409.5 3.3 convolution_add_fusion.4
  415.6 5.5 %collective-permute-start = (bf16[32,1152]{1,0:T(8,128)(2,1)S(1)}, bf16[32,1152]{1,0:T(8,128)(2,1)S(1)}, u32[]{:S(2)}, u32[]{:S(2)}) collective-permute-start(bf16[32,1152]{1,0:T(8,128)(2,1)S(1)} %copy.24), channel_id=1, source_target_pairs={{0,248},{8,0},{16,8},{24,16},{32,24},{40,32},{48,40},{56,48},{64,5... | collective-permute-start | bytes 221192 | tf_op jit(solution)/shard_map/while/body/eval_jaxpr/ppermute | solution.py:25
  424.0 10.6 %collective-permute-done.2 = f32[32,1152]{1,0:T(8,128)S(1)} collective-permute-done((f32[32,1152]{1,0:T(8,128)}, f32[32,1152]{1,0:T(8,128)S(1)}, u32[]{:S(2)}, u32[]{:S(2)}) %collective-permute-start.2) | collective-permute-done | bytes 147488 | tf_op jit(solution)/shard_map/ppermute | solution.py:25
  (91 shorter events, 48.2 us)
Async XLA Ops:
  6.5 264.6 %copy-start = (bf16[1152,1152]{1,0:T(8,128)(2,1)S(1)}, bf16[1152,1152]{1,0:T(8,128)(2,1)}, u32[]{:S(2)}) copy-start(bf16[1152,1152]{1,0:T(8,128)(2,1)} %param.28) | copy-start | bytes 7962628
  6.5 116.0 %all-gather.5.cloned.1.call-start = ((), (), s32[]{:S(2)}) async-start(), calls=%async_computation.1 | async-start | bytes 11280384 | tf_op jit(solution)/shard_map/all_gather | solution.py:60
  7.3 225.6 %all-gather.7.cloned.1.call-start = ((), (), s32[]{:S(2)}) async-start(), calls=%async_computation.2 | async-start | bytes 11280384 | tf_op jit(solution)/shard_map/all_gather | solution.py:68
  134.3 110.5 %copy-start.7 = (f32[4304]{0:T(1024)S(1)}, f32[4304]{0:T(1024)}, u32[]{:S(2)}) copy-start(f32[4304]{0:T(1024)} %param.23) | copy-start | bytes 51652
  134.4 110.5 %copy-start.8 = (f32[1152]{0:T(1024)S(1)}, f32[1152]{0:T(1024)}, u32[]{:S(2)}) copy-start(f32[1152]{0:T(1024)} %param.25) | copy-start | bytes 13828
  134.4 110.5 %copy-start.9 = (f32[1152]{0:T(1024)S(1)}, f32[1152]{0:T(1024)}, u32[]{:S(2)}) copy-start(f32[1152]{0:T(1024)} %param.21) | copy-start | bytes 13828
  134.4 110.5 %copy-start.10 = (f32[1152]{0:T(1024)S(1)}, f32[1152]{0:T(1024)}, u32[]{:S(2)}) copy-start(f32[1152]{0:T(1024)} %param.20) | copy-start | bytes 13828
  244.8 25.3 %copy-start.5 = (f32[1152]{0:T(1024)S(1)}, f32[1152]{0:T(1024)}, u32[]{:S(2)}) copy-start(f32[1152]{0:T(1024)} %param.26) | copy-start | bytes 13828
  272.9 14.4 %all-to-all-start = ((bf16[8,32,1152]{2,1,0:T(8,128)(2,1)}), bf16[8,32,1152]{2,1,0:T(8,128)(2,1)S(1)}, u32[]{:S(2)}, u32[]{:S(2)}) async-start(bf16[8,32,1152]{2,1,0:T(8,128)(2,1)} %broadcast_in_dim.5), calls=%async_computation | async-start | bytes 1179648 | tf_op jit(solution)/shard_map/all_to_all | solution.py:9
  290.7 7.1 %collective-permute-start.1 = (f32[32,1152]{1,0:T(8,128)}, f32[32,1152]{1,0:T(8,128)S(1)}, u32[]{:S(2)}, u32[]{:S(2)}) collective-permute-start(f32[32,1152]{1,0:T(8,128)} %convolution_add_fusion.4), channel_id=1, source_target_pairs={{0,248},{8,0},{16,8},{24,16},{32,24},{40,32},{48,40},{56,48},{64,5... | collective-permute-start | bytes 442376 | tf_op jit(solution)/shard_map/while/body/eval_jaxpr/ppermute | solution.py:25
  291.4 6.3 %collective-permute-start = (bf16[32,1152]{1,0:T(8,128)(2,1)S(1)}, bf16[32,1152]{1,0:T(8,128)(2,1)S(1)}, u32[]{:S(2)}, u32[]{:S(2)}) collective-permute-start(bf16[32,1152]{1,0:T(8,128)(2,1)S(1)} %copy.24), channel_id=1, source_target_pairs={{0,248},{8,0},{16,8},{24,16},{32,24},{40,32},{48,40},{56,48},{64,5... | collective-permute-start | bytes 221192 | tf_op jit(solution)/shard_map/while/body/eval_jaxpr/ppermute | solution.py:25
  301.0 8.6 %collective-permute-start.1 = (f32[32,1152]{1,0:T(8,128)}, f32[32,1152]{1,0:T(8,128)S(1)}, u32[]{:S(2)}, u32[]{:S(2)}) collective-permute-start(f32[32,1152]{1,0:T(8,128)} %convolution_add_fusion.4), channel_id=1, source_target_pairs={{0,248},{8,0},{16,8},{24,16},{32,24},{40,32},{48,40},{56,48},{64,5... | collective-permute-start | bytes 442376 | tf_op jit(solution)/shard_map/while/body/eval_jaxpr/ppermute | solution.py:25
  303.2 6.4 %collective-permute-start = (bf16[32,1152]{1,0:T(8,128)(2,1)S(1)}, bf16[32,1152]{1,0:T(8,128)(2,1)S(1)}, u32[]{:S(2)}, u32[]{:S(2)}) collective-permute-start(bf16[32,1152]{1,0:T(8,128)(2,1)S(1)} %copy.24), channel_id=1, source_target_pairs={{0,248},{8,0},{16,8},{24,16},{32,24},{40,32},{48,40},{56,48},{64,5... | collective-permute-start | bytes 221192 | tf_op jit(solution)/shard_map/while/body/eval_jaxpr/ppermute | solution.py:25
  312.9 9.2 %collective-permute-start.1 = (f32[32,1152]{1,0:T(8,128)}, f32[32,1152]{1,0:T(8,128)S(1)}, u32[]{:S(2)}, u32[]{:S(2)}) collective-permute-start(f32[32,1152]{1,0:T(8,128)} %convolution_add_fusion.4), channel_id=1, source_target_pairs={{0,248},{8,0},{16,8},{24,16},{32,24},{40,32},{48,40},{56,48},{64,5... | collective-permute-start | bytes 442376 | tf_op jit(solution)/shard_map/while/body/eval_jaxpr/ppermute | solution.py:25
  315.7 6.4 %collective-permute-start = (bf16[32,1152]{1,0:T(8,128)(2,1)S(1)}, bf16[32,1152]{1,0:T(8,128)(2,1)S(1)}, u32[]{:S(2)}, u32[]{:S(2)}) collective-permute-start(bf16[32,1152]{1,0:T(8,128)(2,1)S(1)} %copy.24), channel_id=1, source_target_pairs={{0,248},{8,0},{16,8},{24,16},{32,24},{40,32},{48,40},{56,48},{64,5... | collective-permute-start | bytes 221192 | tf_op jit(solution)/shard_map/while/body/eval_jaxpr/ppermute | solution.py:25
  325.4 9.2 %collective-permute-start.1 = (f32[32,1152]{1,0:T(8,128)}, f32[32,1152]{1,0:T(8,128)S(1)}, u32[]{:S(2)}, u32[]{:S(2)}) collective-permute-start(f32[32,1152]{1,0:T(8,128)} %convolution_add_fusion.4), channel_id=1, source_target_pairs={{0,248},{8,0},{16,8},{24,16},{32,24},{40,32},{48,40},{56,48},{64,5... | collective-permute-start | bytes 442376 | tf_op jit(solution)/shard_map/while/body/eval_jaxpr/ppermute | solution.py:25
  328.2 6.4 %collective-permute-start = (bf16[32,1152]{1,0:T(8,128)(2,1)S(1)}, bf16[32,1152]{1,0:T(8,128)(2,1)S(1)}, u32[]{:S(2)}, u32[]{:S(2)}) collective-permute-start(bf16[32,1152]{1,0:T(8,128)(2,1)S(1)} %copy.24), channel_id=1, source_target_pairs={{0,248},{8,0},{16,8},{24,16},{32,24},{40,32},{48,40},{56,48},{64,5... | collective-permute-start | bytes 221192 | tf_op jit(solution)/shard_map/while/body/eval_jaxpr/ppermute | solution.py:25
  337.9 9.2 %collective-permute-start.1 = (f32[32,1152]{1,0:T(8,128)}, f32[32,1152]{1,0:T(8,128)S(1)}, u32[]{:S(2)}, u32[]{:S(2)}) collective-permute-start(f32[32,1152]{1,0:T(8,128)} %convolution_add_fusion.4), channel_id=1, source_target_pairs={{0,248},{8,0},{16,8},{24,16},{32,24},{40,32},{48,40},{56,48},{64,5... | collective-permute-start | bytes 442376 | tf_op jit(solution)/shard_map/while/body/eval_jaxpr/ppermute | solution.py:25
  340.7 6.4 %collective-permute-start = (bf16[32,1152]{1,0:T(8,128)(2,1)S(1)}, bf16[32,1152]{1,0:T(8,128)(2,1)S(1)}, u32[]{:S(2)}, u32[]{:S(2)}) collective-permute-start(bf16[32,1152]{1,0:T(8,128)(2,1)S(1)} %copy.24), channel_id=1, source_target_pairs={{0,248},{8,0},{16,8},{24,16},{32,24},{40,32},{48,40},{56,48},{64,5... | collective-permute-start | bytes 221192 | tf_op jit(solution)/shard_map/while/body/eval_jaxpr/ppermute | solution.py:25
  350.4 9.2 %collective-permute-start.1 = (f32[32,1152]{1,0:T(8,128)}, f32[32,1152]{1,0:T(8,128)S(1)}, u32[]{:S(2)}, u32[]{:S(2)}) collective-permute-start(f32[32,1152]{1,0:T(8,128)} %convolution_add_fusion.4), channel_id=1, source_target_pairs={{0,248},{8,0},{16,8},{24,16},{32,24},{40,32},{48,40},{56,48},{64,5... | collective-permute-start | bytes 442376 | tf_op jit(solution)/shard_map/while/body/eval_jaxpr/ppermute | solution.py:25
  353.1 6.4 %collective-permute-start = (bf16[32,1152]{1,0:T(8,128)(2,1)S(1)}, bf16[32,1152]{1,0:T(8,128)(2,1)S(1)}, u32[]{:S(2)}, u32[]{:S(2)}) collective-permute-start(bf16[32,1152]{1,0:T(8,128)(2,1)S(1)} %copy.24), channel_id=1, source_target_pairs={{0,248},{8,0},{16,8},{24,16},{32,24},{40,32},{48,40},{56,48},{64,5... | collective-permute-start | bytes 221192 | tf_op jit(solution)/shard_map/while/body/eval_jaxpr/ppermute | solution.py:25
  362.9 9.2 %collective-permute-start.1 = (f32[32,1152]{1,0:T(8,128)}, f32[32,1152]{1,0:T(8,128)S(1)}, u32[]{:S(2)}, u32[]{:S(2)}) collective-permute-start(f32[32,1152]{1,0:T(8,128)} %convolution_add_fusion.4), channel_id=1, source_target_pairs={{0,248},{8,0},{16,8},{24,16},{32,24},{40,32},{48,40},{56,48},{64,5... | collective-permute-start | bytes 442376 | tf_op jit(solution)/shard_map/while/body/eval_jaxpr/ppermute | solution.py:25
  365.6 6.4 %collective-permute-start = (bf16[32,1152]{1,0:T(8,128)(2,1)S(1)}, bf16[32,1152]{1,0:T(8,128)(2,1)S(1)}, u32[]{:S(2)}, u32[]{:S(2)}) collective-permute-start(bf16[32,1152]{1,0:T(8,128)(2,1)S(1)} %copy.24), channel_id=1, source_target_pairs={{0,248},{8,0},{16,8},{24,16},{32,24},{40,32},{48,40},{56,48},{64,5... | collective-permute-start | bytes 221192 | tf_op jit(solution)/shard_map/while/body/eval_jaxpr/ppermute | solution.py:25
  375.4 9.2 %collective-permute-start.1 = (f32[32,1152]{1,0:T(8,128)}, f32[32,1152]{1,0:T(8,128)S(1)}, u32[]{:S(2)}, u32[]{:S(2)}) collective-permute-start(f32[32,1152]{1,0:T(8,128)} %convolution_add_fusion.4), channel_id=1, source_target_pairs={{0,248},{8,0},{16,8},{24,16},{32,24},{40,32},{48,40},{56,48},{64,5... | collective-permute-start | bytes 442376 | tf_op jit(solution)/shard_map/while/body/eval_jaxpr/ppermute | solution.py:25
  378.1 6.4 %collective-permute-start = (bf16[32,1152]{1,0:T(8,128)(2,1)S(1)}, bf16[32,1152]{1,0:T(8,128)(2,1)S(1)}, u32[]{:S(2)}, u32[]{:S(2)}) collective-permute-start(bf16[32,1152]{1,0:T(8,128)(2,1)S(1)} %copy.24), channel_id=1, source_target_pairs={{0,248},{8,0},{16,8},{24,16},{32,24},{40,32},{48,40},{56,48},{64,5... | collective-permute-start | bytes 221192 | tf_op jit(solution)/shard_map/while/body/eval_jaxpr/ppermute | solution.py:25
  387.9 9.2 %collective-permute-start.1 = (f32[32,1152]{1,0:T(8,128)}, f32[32,1152]{1,0:T(8,128)S(1)}, u32[]{:S(2)}, u32[]{:S(2)}) collective-permute-start(f32[32,1152]{1,0:T(8,128)} %convolution_add_fusion.4), channel_id=1, source_target_pairs={{0,248},{8,0},{16,8},{24,16},{32,24},{40,32},{48,40},{56,48},{64,5... | collective-permute-start | bytes 442376 | tf_op jit(solution)/shard_map/while/body/eval_jaxpr/ppermute | solution.py:25
  390.6 6.4 %collective-permute-start = (bf16[32,1152]{1,0:T(8,128)(2,1)S(1)}, bf16[32,1152]{1,0:T(8,128)(2,1)S(1)}, u32[]{:S(2)}, u32[]{:S(2)}) collective-permute-start(bf16[32,1152]{1,0:T(8,128)(2,1)S(1)} %copy.24), channel_id=1, source_target_pairs={{0,248},{8,0},{16,8},{24,16},{32,24},{40,32},{48,40},{56,48},{64,5... | collective-permute-start | bytes 221192 | tf_op jit(solution)/shard_map/while/body/eval_jaxpr/ppermute | solution.py:25
  400.3 9.2 %collective-permute-start.1 = (f32[32,1152]{1,0:T(8,128)}, f32[32,1152]{1,0:T(8,128)S(1)}, u32[]{:S(2)}, u32[]{:S(2)}) collective-permute-start(f32[32,1152]{1,0:T(8,128)} %convolution_add_fusion.4), channel_id=1, source_target_pairs={{0,248},{8,0},{16,8},{24,16},{32,24},{40,32},{48,40},{56,48},{64,5... | collective-permute-start | bytes 442376 | tf_op jit(solution)/shard_map/while/body/eval_jaxpr/ppermute | solution.py:25
  403.1 6.4 %collective-permute-start = (bf16[32,1152]{1,0:T(8,128)(2,1)S(1)}, bf16[32,1152]{1,0:T(8,128)(2,1)S(1)}, u32[]{:S(2)}, u32[]{:S(2)}) collective-permute-start(bf16[32,1152]{1,0:T(8,128)(2,1)S(1)} %copy.24), channel_id=1, source_target_pairs={{0,248},{8,0},{16,8},{24,16},{32,24},{40,32},{48,40},{56,48},{64,5... | collective-permute-start | bytes 221192 | tf_op jit(solution)/shard_map/while/body/eval_jaxpr/ppermute | solution.py:25
  412.8 9.2 %collective-permute-start.1 = (f32[32,1152]{1,0:T(8,128)}, f32[32,1152]{1,0:T(8,128)S(1)}, u32[]{:S(2)}, u32[]{:S(2)}) collective-permute-start(f32[32,1152]{1,0:T(8,128)} %convolution_add_fusion.4), channel_id=1, source_target_pairs={{0,248},{8,0},{16,8},{24,16},{32,24},{40,32},{48,40},{56,48},{64,5... | collective-permute-start | bytes 442376 | tf_op jit(solution)/shard_map/while/body/eval_jaxpr/ppermute | solution.py:25
  415.6 6.4 %collective-permute-start = (bf16[32,1152]{1,0:T(8,128)(2,1)S(1)}, bf16[32,1152]{1,0:T(8,128)(2,1)S(1)}, u32[]{:S(2)}, u32[]{:S(2)}) collective-permute-start(bf16[32,1152]{1,0:T(8,128)(2,1)S(1)} %copy.24), channel_id=1, source_target_pairs={{0,248},{8,0},{16,8},{24,16},{32,24},{40,32},{48,40},{56,48},{64,5... | collective-permute-start | bytes 221192 | tf_op jit(solution)/shard_map/while/body/eval_jaxpr/ppermute | solution.py:25
  424.0 10.6 %collective-permute-start.2 = (f32[32,1152]{1,0:T(8,128)}, f32[32,1152]{1,0:T(8,128)S(1)}, u32[]{:S(2)}, u32[]{:S(2)}) collective-permute-start(f32[32,1152]{1,0:T(8,128)} %convolution_add_fusion.1), channel_id=1, source_target_pairs={{0,88},{8,96},{16,104},{24,112},{32,120},{40,128},{48,136},{56,144... | collective-permute-start | bytes 442376 | tf_op jit(solution)/shard_map/ppermute | solution.py:25
  (5 other events, 11.1 us)
Sparse Core Ops, SparseCore 0:
  9.1 113.3 all-gather.4
  124.3 108.5 all-gather.6
where the time goes:
time: 444 us; the launch traced here: 442 us
  waiting for transfers between devices  242 us (55%)
  starting transfers between devices  91.3 us (21%)
  matrix products  62 us (14%)
  local copies, waits for them, and re-layouts  25 us (6%)
  between operations  14.8 us (3%)
  other arithmetic  7.29 us (2%)
    all_gather x1, waiting for transfers between devices, on_device(): lax.all_gather(fc1_weight, 'fsdp', axis=1, tiled=True)  111 us
    all_gather x1, waiting for transfers between devices, on_device(): lax.all_gather(fc2_weight, 'fsdp', axis=0, tiled=True)  98.5 us
    ppermute x23, starting transfers between devices, from_behind(): lax.ppermute(array, axis, [(i, (i + by) % count) for i in range(count)])  87.7 us
    dot_general x12, matrix products, pair_term(): lax.dot_general(weight, units, (((0,), (0,)), ((), ())), preferred_elemen...  38.2 us
    unnamed x24, local copies, waits for them, and re-layouts  23.9 us
    dot_general x1, matrix products, on_device(): jnp.dot(act, lax.all_gather(fc2_weight, 'fsdp', axis=0, tiled=True), pref...  23.1 us
    ppermute x23, waiting for transfers between devices, from_behind(): lax.ppermute(array, axis, [(i, (i + by) % count) for i in range(count)])  21.2 us
    all_to_all x1, waiting for transfers between devices, from_everyone(): return lax.all_to_all(copies, axis, split_axis=0, concat_axis=0, tiled=True)  9.5 us
  transfers between devices with their start and end apart: 26, of which 15 were waited for; matrix products, arithmetic and copies ran while one was open for 3% of the time, Pallas kernels for 0%

commit v1 on v0

--- a/solution.py
+++ b/solution.py
@@ -57,7 +57,7 @@
     pre = (
         jnp.dot(
             normed,
-            lax.all_gather(fc1_weight, "fsdp", axis=1, tiled=True),
+            jnp.concatenate(lax.all_gather(fc1_weight, "fsdp"), axis=1),
             preferred_element_type=jnp.float32,
         )
         + fc1_bias

time: 444 us -> 444 us (level)
  waiting for transfers between devices: 242 us -> 214 us
  local copies, waits for them, and re-layouts: 25 us -> 52.6 us
    all_gather x1, waiting for transfers between devices: 98.5 us -> 70.8 us  [on_device(): lax.all_gather(fc2_weight, 'fsdp', axis=0, tiled=True)]
    all_gather x0 -> x2, local copies, waits for them, and re-layouts: none -> 17.7 us  [on_device(): lax.all_gather(fc1_weight, 'fsdp')]
    reshape x0 -> x1, local copies, waits for them, and re-layouts: none -> 12 us  [on_device(): jnp.concatenate(lax.all_gather(fc1_weight, 'fsdp'), axis=1)]
  transfers between devices with their start and end apart: 26 -> 26, of which waited for: 15 -> 15; matrix products, arithmetic and copies ran while one was open for 3% -> 10% of each run, Pallas kernels for 0% -> 0%
where the time goes in v1:
time: 444 us; the launch traced here: 442 us
  waiting for transfers between devices  214 us (48%)
  starting transfers between devices  91.3 us (21%)
  matrix products  62 us (14%)
  local copies, waits for them, and re-layouts  52.6 us (12%)
  between operations  14.8 us (3%)
  other arithmetic  7.29 us (2%)
    all_gather x1, waiting for transfers between devices, on_device(): lax.all_gather(fc1_weight, 'fsdp')  111 us
    ppermute x23, starting transfers between devices, from_behind(): lax.ppermute(array, axis, [(i, (i + by) % count) for i in range(count)])  87.7 us
    all_gather x1, waiting for transfers between devices, on_device(): lax.all_gather(fc2_weight, 'fsdp', axis=0, tiled=True)  70.8 us
    dot_general x12, matrix products, pair_term(): lax.dot_general(weight, units, (((0,), (0,)), ((), ())), preferred_elemen...  38.2 us
    dot_general x1, matrix products, on_device(): jnp.dot(act, lax.all_gather(fc2_weight, 'fsdp', axis=0, tiled=True), pref...  23.1 us
    unnamed x24, local copies, waits for them, and re-layouts  21.9 us
    ppermute x23, waiting for transfers between devices, from_behind(): lax.ppermute(array, axis, [(i, (i + by) % count) for i in range(count)])  21.2 us
    all_gather x2, local copies, waits for them, and re-layouts, on_device(): lax.all_gather(fc1_weight, 'fsdp')  17.7 us
  transfers between devices with their start and end apart: 26, of which 15 were waited for; matrix products, arithmetic and copies ran while one was open for 10% of the time, Pallas kernels for 0%

profile of v1, /device:TPU:1, one launch (start us, length us, event | category | flops | bytes accessed | tf_op | source)
XLA Modules:
  0.0 442.0 jit_solution(16784996015665665445)
XLA Ops:
  11.5 111.0 %all-gather.5.cloned.1.call-done = bf16[9216,538]{0,1:T(8,128)(2,1)} async-done(((bf16[1152,538]{0,1:T(8,128)(2,1)}), bf16[9216,538]{0,1:T(8,128)(2,1)}) %all-gather.5.cloned.1.call-update) | async-done | bytes 9916432 | tf_op jit(solution)/shard_map/all_gather | solution.py:60
  122.5 9.9 %copy.22 = bf16[68,8,8,1152]{3,2,1,0:T(8,128)(2,1)} copy(bf16[68,8,8,1152]{3,1,2,0:T(8,128)(2,1)} %bitcast.50) | data formatting | bytes 20054016
  132.5 8.7 %slice_bitcast_fusion = bf16[8,1152,538]{1,0,2:T(8,128)(2,1)} fusion(bf16[544,8,1152]{2,1,0:T(8,128)(2,1)} %bitcast.49), kind=kLoop, calls=%fused_computation.24 | loop fusion | bytes 19832832 | tf_op jit(solution)/shard_map/all_gather | solution.py:60
  141.2 8.9 %copy.24 = bf16[8,1152,538]{1,2,0:T(8,128)(2,1)} copy(bf16[8,1152,538]{1,0,2:T(8,128)(2,1)} %slice_bitcast_fusion) | data formatting | bytes 19832832 | tf_op jit(solution)/shard_map/all_gather | solution.py:60
  150.1 12.0 %reshape.68 = bf16[1152,4304]{0,1:T(8,128)(2,1)} reshape(bf16[1152,8,538]{0,2,1:T(8,128)(2,1)} %bitcast.48) | data formatting | bytes 19832832 | tf_op jit(solution)/shard_map/reshape | solution.py:60
  162.2 70.8 %all-gather.7.cloned.1.call-done = bf16[8,538,1152]{2,1,0:T(8,128)(2,1)} async-done(((bf16[1,538,1152]{2,1,0:T(8,128)(2,1)}), bf16[8,538,1152]{2,1,0:T(8,128)(2,1)}) %all-gather.7.cloned.1.call-update) | async-done | bytes 9916432 | tf_op jit(solution)/shard_map/all_gather | solution.py:68
  232.9 11.8 %reshape.77 = bf16[4304,1152]{1,0:T(8,128)(2,1)} reshape(bf16[8,538,1152]{2,1,0:T(8,128)(2,1)} %all-gather.7.cloned.1.call-done) | data formatting | bytes 19832832
  244.8 23.1 %fusion.72 = (f32[512]{0:T(512)S(1)}, f32[512,1152]{1,0:T(8,128)}) fusion(f32[1152]{0:T(1024)S(1)} %copy-done.8, bf16[4304,1152]{1,0:T(8,128)(2,1)} %reshape.77, bf16[1152,4304]{0,1:T(8,128)(2,1)} %reshape.68, f32[4304]{0:T(1024)S(1)} %copy-done.7, bf16[512,1152]{1,0:T(8,128)(2,1)} %param.18, f32[1152]{0:T(1024)S(1)} %copy-done.9, f32[1152]{0:T(1024)S(1)} %copy-done.10, ...), kind=kOutput, calls=%fused_computation.93 | convolution fusion | flops 10182344704 | bytes 23408960 | tf_op jit(solution)/shard_map/dot_general | solution.py:66
  272.8 3.5 all-to-all-start
  277.8 9.5 %all-to-all-done = bf16[8,32,1152]{2,1,0:T(8,128)(2,1)S(1)} async-done(((bf16[8,32,1152]{2,1,0:T(8,128)(2,1)}), bf16[8,32,1152]{2,1,0:T(8,128)(2,1)S(1)}, u32[]{:S(2)}, u32[]{:S(2)}) %all-to-all-start) | async-done | bytes 589856 | tf_op jit(solution)/shard_map/all_to_all | solution.py:9
  287.3 134.7 %while.15 = (s32[]{:T(128)}, bf16[32,1152]{1,0:T(8,128)(2,1)S(1)}, f32[32,1152]{1,0:T(8,128)S(1)}, f32[]{:T(128)}, bf16[256,1152]{1,0:T(8,128)(2,1)S(1)}, /*inde...) while((s32[]{:T(128)}, bf16[32,1152]{1,0:T(8,128)(2,1)S(1)}, f32[32,1152]{1,0:T(8,128)S(1)}, f32[]{:T(128)}, ...), condition=%wide.region_9.10_spmd, body=%wide.region_8.9_spmd.sunk | while | flops 37875712 | bytes 2598565 | solution.py:117
  287.3 3.3 convolution_add_fusion.4
  291.4 4.8 %collective-permute-start = (bf16[32,1152]{1,0:T(8,128)(2,1)S(1)}, bf16[32,1152]{1,0:T(8,128)(2,1)S(1)}, u32[]{:S(2)}, u32[]{:S(2)}) collective-permute-start(bf16[32,1152]{1,0:T(8,128)(2,1)S(1)} %copy.29), channel_id=1, source_target_pairs={{0,248},{8,0},{16,8},{24,16},{32,24},{40,32},{48,40},{56,48},{64,5... | collective-permute-start | bytes 221192 | tf_op jit(solution)/shard_map/while/body/eval_jaxpr/ppermute | solution.py:25
  297.7 3.3 convolution_add_fusion.4
  303.1 5.5 %collective-permute-start = (bf16[32,1152]{1,0:T(8,128)(2,1)S(1)}, bf16[32,1152]{1,0:T(8,128)(2,1)S(1)}, u32[]{:S(2)}, u32[]{:S(2)}) collective-permute-start(bf16[32,1152]{1,0:T(8,128)(2,1)S(1)} %copy.29), channel_id=1, source_target_pairs={{0,248},{8,0},{16,8},{24,16},{32,24},{40,32},{48,40},{56,48},{64,5... | collective-permute-start | bytes 221192 | tf_op jit(solution)/shard_map/while/body/eval_jaxpr/ppermute | solution.py:25
  309.6 3.3 convolution_add_fusion.4
  315.6 5.5 %collective-permute-start = (bf16[32,1152]{1,0:T(8,128)(2,1)S(1)}, bf16[32,1152]{1,0:T(8,128)(2,1)S(1)}, u32[]{:S(2)}, u32[]{:S(2)}) collective-permute-start(bf16[32,1152]{1,0:T(8,128)(2,1)S(1)} %copy.29), channel_id=1, source_target_pairs={{0,248},{8,0},{16,8},{24,16},{32,24},{40,32},{48,40},{56,48},{64,5... | collective-permute-start | bytes 221192 | tf_op jit(solution)/shard_map/while/body/eval_jaxpr/ppermute | solution.py:25
  322.1 3.3 convolution_add_fusion.4
  328.1 5.5 %collective-permute-start = (bf16[32,1152]{1,0:T(8,128)(2,1)S(1)}, bf16[32,1152]{1,0:T(8,128)(2,1)S(1)}, u32[]{:S(2)}, u32[]{:S(2)}) collective-permute-start(bf16[32,1152]{1,0:T(8,128)(2,1)S(1)} %copy.29), channel_id=1, source_target_pairs={{0,248},{8,0},{16,8},{24,16},{32,24},{40,32},{48,40},{56,48},{64,5... | collective-permute-start | bytes 221192 | tf_op jit(solution)/shard_map/while/body/eval_jaxpr/ppermute | solution.py:25
  334.6 3.3 convolution_add_fusion.4
  340.6 5.5 %collective-permute-start = (bf16[32,1152]{1,0:T(8,128)(2,1)S(1)}, bf16[32,1152]{1,0:T(8,128)(2,1)S(1)}, u32[]{:S(2)}, u32[]{:S(2)}) collective-permute-start(bf16[32,1152]{1,0:T(8,128)(2,1)S(1)} %copy.29), channel_id=1, source_target_pairs={{0,248},{8,0},{16,8},{24,16},{32,24},{40,32},{48,40},{56,48},{64,5... | collective-permute-start | bytes 221192 | tf_op jit(solution)/shard_map/while/body/eval_jaxpr/ppermute | solution.py:25
  347.0 3.3 convolution_add_fusion.4
  353.1 5.5 %collective-permute-start = (bf16[32,1152]{1,0:T(8,128)(2,1)S(1)}, bf16[32,1152]{1,0:T(8,128)(2,1)S(1)}, u32[]{:S(2)}, u32[]{:S(2)}) collective-permute-start(bf16[32,1152]{1,0:T(8,128)(2,1)S(1)} %copy.29), channel_id=1, source_target_pairs={{0,248},{8,0},{16,8},{24,16},{32,24},{40,32},{48,40},{56,48},{64,5... | collective-permute-start | bytes 221192 | tf_op jit(solution)/shard_map/while/body/eval_jaxpr/ppermute | solution.py:25
  359.5 3.3 convolution_add_fusion.4
  365.6 5.5 %collective-permute-start = (bf16[32,1152]{1,0:T(8,128)(2,1)S(1)}, bf16[32,1152]{1,0:T(8,128)(2,1)S(1)}, u32[]{:S(2)}, u32[]{:S(2)}) collective-permute-start(bf16[32,1152]{1,0:T(8,128)(2,1)S(1)} %copy.29), channel_id=1, source_target_pairs={{0,248},{8,0},{16,8},{24,16},{32,24},{40,32},{48,40},{56,48},{64,5... | collective-permute-start | bytes 221192 | tf_op jit(solution)/shard_map/while/body/eval_jaxpr/ppermute | solution.py:25
  378.0 5.5 %collective-permute-start = (bf16[32,1152]{1,0:T(8,128)(2,1)S(1)}, bf16[32,1152]{1,0:T(8,128)(2,1)S(1)}, u32[]{:S(2)}, u32[]{:S(2)}) collective-permute-start(bf16[32,1152]{1,0:T(8,128)(2,1)S(1)} %copy.29), channel_id=1, source_target_pairs={{0,248},{8,0},{16,8},{24,16},{32,24},{40,32},{48,40},{56,48},{64,5... | collective-permute-start | bytes 221192 | tf_op jit(solution)/shard_map/while/body/eval_jaxpr/ppermute | solution.py:25
  390.5 5.5 %collective-permute-start = (bf16[32,1152]{1,0:T(8,128)(2,1)S(1)}, bf16[32,1152]{1,0:T(8,128)(2,1)S(1)}, u32[]{:S(2)}, u32[]{:S(2)}) collective-permute-start(bf16[32,1152]{1,0:T(8,128)(2,1)S(1)} %copy.29), channel_id=1, source_target_pairs={{0,248},{8,0},{16,8},{24,16},{32,24},{40,32},{48,40},{56,48},{64,5... | collective-permute-start | bytes 221192 | tf_op jit(solution)/shard_map/while/body/eval_jaxpr/ppermute | solution.py:25
  397.0 3.3 convolution_add_fusion.4
  403.0 5.5 %collective-permute-start = (bf16[32,1152]{1,0:T(8,128)(2,1)S(1)}, bf16[32,1152]{1,0:T(8,128)(2,1)S(1)}, u32[]{:S(2)}, u32[]{:S(2)}) collective-permute-start(bf16[32,1152]{1,0:T(8,128)(2,1)S(1)} %copy.29), channel_id=1, source_target_pairs={{0,248},{8,0},{16,8},{24,16},{32,24},{40,32},{48,40},{56,48},{64,5... | collective-permute-start | bytes 221192 | tf_op jit(solution)/shard_map/while/body/eval_jaxpr/ppermute | solution.py:25
  409.5 3.3 convolution_add_fusion.4
  415.5 5.5 %collective-permute-start = (bf16[32,1152]{1,0:T(8,128)(2,1)S(1)}, bf16[32,1152]{1,0:T(8,128)(2,1)S(1)}, u32[]{:S(2)}, u32[]{:S(2)}) collective-permute-start(bf16[32,1152]{1,0:T(8,128)(2,1)S(1)} %copy.29), channel_id=1, source_target_pairs={{0,248},{8,0},{16,8},{24,16},{32,24},{40,32},{48,40},{56,48},{64,5... | collective-permute-start | bytes 221192 | tf_op jit(solution)/shard_map/while/body/eval_jaxpr/ppermute | solution.py:25
  423.9 10.6 %collective-permute-done.2 = f32[32,1152]{1,0:T(8,128)S(1)} collective-permute-done((f32[32,1152]{1,0:T(8,128)}, f32[32,1152]{1,0:T(8,128)S(1)}, u32[]{:S(2)}, u32[]{:S(2)}) %collective-permute-start.2) | collective-permute-done | bytes 147488 | tf_op jit(solution)/shard_map/ppermute | solution.py:25
  (94 shorter events, 57.6 us)
Async XLA Ops:
  6.5 264.6 %copy-start = (bf16[1152,1152]{1,0:T(8,128)(2,1)S(1)}, bf16[1152,1152]{1,0:T(8,128)(2,1)}, u32[]{:S(2)}) copy-start(bf16[1152,1152]{1,0:T(8,128)(2,1)} %param.28) | copy-start | bytes 7962628
  6.5 116.0 %all-gather.5.cloned.1.call-start = ((), (), s32[]{:S(2)}) async-start(), calls=%async_computation.1 | async-start | bytes 11280384 | tf_op jit(solution)/shard_map/all_gather | solution.py:60
  7.3 225.6 %all-gather.7.cloned.1.call-start = ((), (), s32[]{:S(2)}) async-start(), calls=%async_computation.2 | async-start | bytes 11280384 | tf_op jit(solution)/shard_map/all_gather | solution.py:68
  162.1 82.6 %copy-start.7 = (f32[4304]{0:T(1024)S(1)}, f32[4304]{0:T(1024)}, u32[]{:S(2)}) copy-start(f32[4304]{0:T(1024)} %param.23) | copy-start | bytes 51652
  162.1 82.6 %copy-start.8 = (f32[1152]{0:T(1024)S(1)}, f32[1152]{0:T(1024)}, u32[]{:S(2)}) copy-start(f32[1152]{0:T(1024)} %param.25) | copy-start | bytes 13828
  162.1 82.6 %copy-start.9 = (f32[1152]{0:T(1024)S(1)}, f32[1152]{0:T(1024)}, u32[]{:S(2)}) copy-start(f32[1152]{0:T(1024)} %param.21) | copy-start | bytes 13828
  162.1 82.6 %copy-start.10 = (f32[1152]{0:T(1024)S(1)}, f32[1152]{0:T(1024)}, u32[]{:S(2)}) copy-start(f32[1152]{0:T(1024)} %param.20) | copy-start | bytes 13828
  244.7 25.3 %copy-start.5 = (f32[1152]{0:T(1024)S(1)}, f32[1152]{0:T(1024)}, u32[]{:S(2)}) copy-start(f32[1152]{0:T(1024)} %param.26) | copy-start | bytes 13828
  272.8 14.4 %all-to-all-start = ((bf16[8,32,1152]{2,1,0:T(8,128)(2,1)}), bf16[8,32,1152]{2,1,0:T(8,128)(2,1)S(1)}, u32[]{:S(2)}, u32[]{:S(2)}) async-start(bf16[8,32,1152]{2,1,0:T(8,128)(2,1)} %broadcast_in_dim.5), calls=%async_computation | async-start | bytes 1179648 | tf_op jit(solution)/shard_map/all_to_all | solution.py:9
  290.6 7.1 %collective-permute-start.1 = (f32[32,1152]{1,0:T(8,128)}, f32[32,1152]{1,0:T(8,128)S(1)}, u32[]{:S(2)}, u32[]{:S(2)}) collective-permute-start(f32[32,1152]{1,0:T(8,128)} %convolution_add_fusion.4), channel_id=1, source_target_pairs={{0,248},{8,0},{16,8},{24,16},{32,24},{40,32},{48,40},{56,48},{64,5... | collective-permute-start | bytes 442376 | tf_op jit(solution)/shard_map/while/body/eval_jaxpr/ppermute | solution.py:25
  291.4 6.3 %collective-permute-start = (bf16[32,1152]{1,0:T(8,128)(2,1)S(1)}, bf16[32,1152]{1,0:T(8,128)(2,1)S(1)}, u32[]{:S(2)}, u32[]{:S(2)}) collective-permute-start(bf16[32,1152]{1,0:T(8,128)(2,1)S(1)} %copy.29), channel_id=1, source_target_pairs={{0,248},{8,0},{16,8},{24,16},{32,24},{40,32},{48,40},{56,48},{64,5... | collective-permute-start | bytes 221192 | tf_op jit(solution)/shard_map/while/body/eval_jaxpr/ppermute | solution.py:25
  301.0 8.6 %collective-permute-start.1 = (f32[32,1152]{1,0:T(8,128)}, f32[32,1152]{1,0:T(8,128)S(1)}, u32[]{:S(2)}, u32[]{:S(2)}) collective-permute-start(f32[32,1152]{1,0:T(8,128)} %convolution_add_fusion.4), channel_id=1, source_target_pairs={{0,248},{8,0},{16,8},{24,16},{32,24},{40,32},{48,40},{56,48},{64,5... | collective-permute-start | bytes 442376 | tf_op jit(solution)/shard_map/while/body/eval_jaxpr/ppermute | solution.py:25
  303.1 6.4 %collective-permute-start = (bf16[32,1152]{1,0:T(8,128)(2,1)S(1)}, bf16[32,1152]{1,0:T(8,128)(2,1)S(1)}, u32[]{:S(2)}, u32[]{:S(2)}) collective-permute-start(bf16[32,1152]{1,0:T(8,128)(2,1)S(1)} %copy.29), channel_id=1, source_target_pairs={{0,248},{8,0},{16,8},{24,16},{32,24},{40,32},{48,40},{56,48},{64,5... | collective-permute-start | bytes 221192 | tf_op jit(solution)/shard_map/while/body/eval_jaxpr/ppermute | solution.py:25
  312.9 9.2 %collective-permute-start.1 = (f32[32,1152]{1,0:T(8,128)}, f32[32,1152]{1,0:T(8,128)S(1)}, u32[]{:S(2)}, u32[]{:S(2)}) collective-permute-start(f32[32,1152]{1,0:T(8,128)} %convolution_add_fusion.4), channel_id=1, source_target_pairs={{0,248},{8,0},{16,8},{24,16},{32,24},{40,32},{48,40},{56,48},{64,5... | collective-permute-start | bytes 442376 | tf_op jit(solution)/shard_map/while/body/eval_jaxpr/ppermute | solution.py:25
  315.6 6.4 %collective-permute-start = (bf16[32,1152]{1,0:T(8,128)(2,1)S(1)}, bf16[32,1152]{1,0:T(8,128)(2,1)S(1)}, u32[]{:S(2)}, u32[]{:S(2)}) collective-permute-start(bf16[32,1152]{1,0:T(8,128)(2,1)S(1)} %copy.29), channel_id=1, source_target_pairs={{0,248},{8,0},{16,8},{24,16},{32,24},{40,32},{48,40},{56,48},{64,5... | collective-permute-start | bytes 221192 | tf_op jit(solution)/shard_map/while/body/eval_jaxpr/ppermute | solution.py:25
  325.4 9.2 %collective-permute-start.1 = (f32[32,1152]{1,0:T(8,128)}, f32[32,1152]{1,0:T(8,128)S(1)}, u32[]{:S(2)}, u32[]{:S(2)}) collective-permute-start(f32[32,1152]{1,0:T(8,128)} %convolution_add_fusion.4), channel_id=1, source_target_pairs={{0,248},{8,0},{16,8},{24,16},{32,24},{40,32},{48,40},{56,48},{64,5... | collective-permute-start | bytes 442376 | tf_op jit(solution)/shard_map/while/body/eval_jaxpr/ppermute | solution.py:25
  328.1 6.4 %collective-permute-start = (bf16[32,1152]{1,0:T(8,128)(2,1)S(1)}, bf16[32,1152]{1,0:T(8,128)(2,1)S(1)}, u32[]{:S(2)}, u32[]{:S(2)}) collective-permute-start(bf16[32,1152]{1,0:T(8,128)(2,1)S(1)} %copy.29), channel_id=1, source_target_pairs={{0,248},{8,0},{16,8},{24,16},{32,24},{40,32},{48,40},{56,48},{64,5... | collective-permute-start | bytes 221192 | tf_op jit(solution)/shard_map/while/body/eval_jaxpr/ppermute | solution.py:25
  337.8 9.2 %collective-permute-start.1 = (f32[32,1152]{1,0:T(8,128)}, f32[32,1152]{1,0:T(8,128)S(1)}, u32[]{:S(2)}, u32[]{:S(2)}) collective-permute-start(f32[32,1152]{1,0:T(8,128)} %convolution_add_fusion.4), channel_id=1, source_target_pairs={{0,248},{8,0},{16,8},{24,16},{32,24},{40,32},{48,40},{56,48},{64,5... | collective-permute-start | bytes 442376 | tf_op jit(solution)/shard_map/while/body/eval_jaxpr/ppermute | solution.py:25
  340.6 6.4 %collective-permute-start = (bf16[32,1152]{1,0:T(8,128)(2,1)S(1)}, bf16[32,1152]{1,0:T(8,128)(2,1)S(1)}, u32[]{:S(2)}, u32[]{:S(2)}) collective-permute-start(bf16[32,1152]{1,0:T(8,128)(2,1)S(1)} %copy.29), channel_id=1, source_target_pairs={{0,248},{8,0},{16,8},{24,16},{32,24},{40,32},{48,40},{56,48},{64,5... | collective-permute-start | bytes 221192 | tf_op jit(solution)/shard_map/while/body/eval_jaxpr/ppermute | solution.py:25
  350.3 9.2 %collective-permute-start.1 = (f32[32,1152]{1,0:T(8,128)}, f32[32,1152]{1,0:T(8,128)S(1)}, u32[]{:S(2)}, u32[]{:S(2)}) collective-permute-start(f32[32,1152]{1,0:T(8,128)} %convolution_add_fusion.4), channel_id=1, source_target_pairs={{0,248},{8,0},{16,8},{24,16},{32,24},{40,32},{48,40},{56,48},{64,5... | collective-permute-start | bytes 442376 | tf_op jit(solution)/shard_map/while/body/eval_jaxpr/ppermute | solution.py:25
  353.1 6.4 %collective-permute-start = (bf16[32,1152]{1,0:T(8,128)(2,1)S(1)}, bf16[32,1152]{1,0:T(8,128)(2,1)S(1)}, u32[]{:S(2)}, u32[]{:S(2)}) collective-permute-start(bf16[32,1152]{1,0:T(8,128)(2,1)S(1)} %copy.29), channel_id=1, source_target_pairs={{0,248},{8,0},{16,8},{24,16},{32,24},{40,32},{48,40},{56,48},{64,5... | collective-permute-start | bytes 221192 | tf_op jit(solution)/shard_map/while/body/eval_jaxpr/ppermute | solution.py:25
  362.8 9.2 %collective-permute-start.1 = (f32[32,1152]{1,0:T(8,128)}, f32[32,1152]{1,0:T(8,128)S(1)}, u32[]{:S(2)}, u32[]{:S(2)}) collective-permute-start(f32[32,1152]{1,0:T(8,128)} %convolution_add_fusion.4), channel_id=1, source_target_pairs={{0,248},{8,0},{16,8},{24,16},{32,24},{40,32},{48,40},{56,48},{64,5... | collective-permute-start | bytes 442376 | tf_op jit(solution)/shard_map/while/body/eval_jaxpr/ppermute | solution.py:25
  365.6 6.4 %collective-permute-start = (bf16[32,1152]{1,0:T(8,128)(2,1)S(1)}, bf16[32,1152]{1,0:T(8,128)(2,1)S(1)}, u32[]{:S(2)}, u32[]{:S(2)}) collective-permute-start(bf16[32,1152]{1,0:T(8,128)(2,1)S(1)} %copy.29), channel_id=1, source_target_pairs={{0,248},{8,0},{16,8},{24,16},{32,24},{40,32},{48,40},{56,48},{64,5... | collective-permute-start | bytes 221192 | tf_op jit(solution)/shard_map/while/body/eval_jaxpr/ppermute | solution.py:25
  375.3 9.2 %collective-permute-start.1 = (f32[32,1152]{1,0:T(8,128)}, f32[32,1152]{1,0:T(8,128)S(1)}, u32[]{:S(2)}, u32[]{:S(2)}) collective-permute-start(f32[32,1152]{1,0:T(8,128)} %convolution_add_fusion.4), channel_id=1, source_target_pairs={{0,248},{8,0},{16,8},{24,16},{32,24},{40,32},{48,40},{56,48},{64,5... | collective-permute-start | bytes 442376 | tf_op jit(solution)/shard_map/while/body/eval_jaxpr/ppermute | solution.py:25
  378.0 6.4 %collective-permute-start = (bf16[32,1152]{1,0:T(8,128)(2,1)S(1)}, bf16[32,1152]{1,0:T(8,128)(2,1)S(1)}, u32[]{:S(2)}, u32[]{:S(2)}) collective-permute-start(bf16[32,1152]{1,0:T(8,128)(2,1)S(1)} %copy.29), channel_id=1, source_target_pairs={{0,248},{8,0},{16,8},{24,16},{32,24},{40,32},{48,40},{56,48},{64,5... | collective-permute-start | bytes 221192 | tf_op jit(solution)/shard_map/while/body/eval_jaxpr/ppermute | solution.py:25
  387.8 9.2 %collective-permute-start.1 = (f32[32,1152]{1,0:T(8,128)}, f32[32,1152]{1,0:T(8,128)S(1)}, u32[]{:S(2)}, u32[]{:S(2)}) collective-permute-start(f32[32,1152]{1,0:T(8,128)} %convolution_add_fusion.4), channel_id=1, source_target_pairs={{0,248},{8,0},{16,8},{24,16},{32,24},{40,32},{48,40},{56,48},{64,5... | collective-permute-start | bytes 442376 | tf_op jit(solution)/shard_map/while/body/eval_jaxpr/ppermute | solution.py:25
  390.5 6.4 %collective-permute-start = (bf16[32,1152]{1,0:T(8,128)(2,1)S(1)}, bf16[32,1152]{1,0:T(8,128)(2,1)S(1)}, u32[]{:S(2)}, u32[]{:S(2)}) collective-permute-start(bf16[32,1152]{1,0:T(8,128)(2,1)S(1)} %copy.29), channel_id=1, source_target_pairs={{0,248},{8,0},{16,8},{24,16},{32,24},{40,32},{48,40},{56,48},{64,5... | collective-permute-start | bytes 221192 | tf_op jit(solution)/shard_map/while/body/eval_jaxpr/ppermute | solution.py:25
  400.3 9.2 %collective-permute-start.1 = (f32[32,1152]{1,0:T(8,128)}, f32[32,1152]{1,0:T(8,128)S(1)}, u32[]{:S(2)}, u32[]{:S(2)}) collective-permute-start(f32[32,1152]{1,0:T(8,128)} %convolution_add_fusion.4), channel_id=1, source_target_pairs={{0,248},{8,0},{16,8},{24,16},{32,24},{40,32},{48,40},{56,48},{64,5... | collective-permute-start | bytes 442376 | tf_op jit(solution)/shard_map/while/body/eval_jaxpr/ppermute | solution.py:25
  403.0 6.4 %collective-permute-start = (bf16[32,1152]{1,0:T(8,128)(2,1)S(1)}, bf16[32,1152]{1,0:T(8,128)(2,1)S(1)}, u32[]{:S(2)}, u32[]{:S(2)}) collective-permute-start(bf16[32,1152]{1,0:T(8,128)(2,1)S(1)} %copy.29), channel_id=1, source_target_pairs={{0,248},{8,0},{16,8},{24,16},{32,24},{40,32},{48,40},{56,48},{64,5... | collective-permute-start | bytes 221192 | tf_op jit(solution)/shard_map/while/body/eval_jaxpr/ppermute | solution.py:25
  412.8 9.2 %collective-permute-start.1 = (f32[32,1152]{1,0:T(8,128)}, f32[32,1152]{1,0:T(8,128)S(1)}, u32[]{:S(2)}, u32[]{:S(2)}) collective-permute-start(f32[32,1152]{1,0:T(8,128)} %convolution_add_fusion.4), channel_id=1, source_target_pairs={{0,248},{8,0},{16,8},{24,16},{32,24},{40,32},{48,40},{56,48},{64,5... | collective-permute-start | bytes 442376 | tf_op jit(solution)/shard_map/while/body/eval_jaxpr/ppermute | solution.py:25
  415.5 6.4 %collective-permute-start = (bf16[32,1152]{1,0:T(8,128)(2,1)S(1)}, bf16[32,1152]{1,0:T(8,128)(2,1)S(1)}, u32[]{:S(2)}, u32[]{:S(2)}) collective-permute-start(bf16[32,1152]{1,0:T(8,128)(2,1)S(1)} %copy.29), channel_id=1, source_target_pairs={{0,248},{8,0},{16,8},{24,16},{32,24},{40,32},{48,40},{56,48},{64,5... | collective-permute-start | bytes 221192 | tf_op jit(solution)/shard_map/while/body/eval_jaxpr/ppermute | solution.py:25
  423.9 10.6 %collective-permute-start.2 = (f32[32,1152]{1,0:T(8,128)}, f32[32,1152]{1,0:T(8,128)S(1)}, u32[]{:S(2)}, u32[]{:S(2)}) collective-permute-start(f32[32,1152]{1,0:T(8,128)} %convolution_add_fusion.1), channel_id=1, source_target_pairs={{0,88},{8,96},{16,104},{24,112},{32,120},{40,128},{48,136},{56,144... | collective-permute-start | bytes 442376 | tf_op jit(solution)/shard_map/ppermute | solution.py:25
  (5 other events, 11.1 us)
Sparse Core Ops, SparseCore 0:
  9.1 113.3 all-gather.4
  124.3 108.5 all-gather.6
